TPU v7x, 512 devices: a whole 4x8x8 slice. The times are simulated.
512 devices in a mesh: tm: 32 (over y, x), blk: 16 (over z, core).
Axes of the slice: x: 4, y: 8, z: 8, core: 2. Of those that a mesh axis runs over, the one named last changes fastest.
Arguments:
- panel_strip: bfloat16 [32, 8192, 2304], P('tm', 'blk'), may hold values from -6 to 6
- pivot_inverses: bfloat16 [32, 2, 256, 256], P('tm'), may hold values from -0.0234375 to 0.0234375
- coupling: float32 [32, 256, 256], P('tm'), may hold values from -0.375 to 0.375
- pivot_nodes: int32 [3, 256], replicated, may hold values from 0 to 8191, as said below
Outputs:
- trailing: bfloat16 [32, 8192, 1792], P('tm', 'blk')
- reduced: float32 [32, 256, 256], P('tm')
Inputs may be any that keep to these rules, and one draw needn't show every extreme that they name: `pivot_nodes`: entry j of every row is a node of the range [(j // 16) * 512, (j // 16 + 1) * 512); all 768 entries differ.
All inputs are finite; a program needn't handle non-finite values.
Results may differ from a plain program's by a relative error of at most 0.0068.
Values may be sent and summed in bfloat16 or wider, within the bound.
No kernel may reach another device: no remote copies, remote signals or barrier semaphores. Data moves between devices by JAX's collectives and lax.ppermute only.
A program may use at most 128 MiB of HBM per device.

v0:
```python
import jax
import jax.numpy as jnp
from jax import lax
from jax.sharding import PartitionSpec as P


def passed_along(x, axis, by):
    count = lax.axis_size(axis)
    return lax.ppermute(x, axis, [(i, i + by) for i in range(count - by)])


def matmul_high(left, right):
    return jnp.dot(left, right, precision=lax.Precision.HIGHEST, preferred_element_type=jnp.float32)


def rounded_dot(left, right):
    return jnp.dot(left, right, preferred_element_type=jnp.float32).astype(jnp.bfloat16)


def reduced_by(block, factor, rows):
    product = jnp.dot(factor, rows, preferred_element_type=jnp.float32)
    return (block.astype(jnp.float32) - product).astype(jnp.bfloat16)


def body(panel_strip, pivot_inverses, coupling, pivot_nodes):
    strip = panel_strip[0]
    first_inverse, second_inverse = (pivot_inverses[0, 0], pivot_inverses[0, 1])
    coupling_here = coupling[0]
    w = coupling_here.shape[0]
    rows_here = strip.shape[0]
    per_device = w // lax.axis_size("blk")
    my_index = lax.axis_index("blk")
    local_rows = (
        lax.dynamic_slice_in_dim(pivot_nodes, my_index * per_device, per_device, 1)
        - my_index * rows_here
    ).reshape(-1)
    picker = (
        local_rows[:, None] == lax.broadcasted_iota(jnp.int32, (3 * per_device, rows_here), 1)
    ).astype(jnp.bfloat16)
    picked = rounded_dot(picker, strip)
    rows_one, rows_two, rows_edge = (
        picked[i * per_device : (i + 1) * per_device] for i in range(3)
    )
    near = lax.all_gather(
        jnp.concatenate(
            [
                rows_one[:, w : 3 * w],
                rows_two[:, :w],
                rows_two[:, 2 * w : 3 * w],
                rows_edge[:, : 3 * w],
            ],
            1,
        ),
        "blk",
        axis=0,
        tiled=True,
    )
    far = lax.all_gather(
        jnp.concatenate([rows_one[:, 3 * w :], rows_two[:, 3 * w :]], 1), "blk", axis=0, tiled=True
    )
    one_next, one_edge = (near[:, :w], near[:, w : 2 * w])
    two_panel, two_edge = (near[:, 2 * w : 3 * w], near[:, 3 * w : 4 * w])
    edge = near[:, 4 * w :]
    factor_at_two = rounded_dot(two_panel, first_inverse)
    factor_at_edge = rounded_dot(edge[:, :w], first_inverse)
    second_edge = reduced_by(two_edge, factor_at_two, one_edge)
    edge_updated = reduced_by(edge[:, w:], factor_at_edge, near[:, : 2 * w])
    edge_factor_two = rounded_dot(edge_updated[:, :w], second_inverse)
    boundary = reduced_by(edge_updated[:, w:], edge_factor_two, second_edge)
    count = lax.axis_size("tm")
    span = coupling_here
    current = boundary.astype(jnp.float32)
    step = 1
    while step < count:
        incoming = passed_along(current.astype(jnp.bfloat16), "tm", step).astype(jnp.float32)
        current = matmul_high(matmul_high(span, incoming), span.T) + current
        if 2 * step < count:
            span = matmul_high(span, passed_along(span, "tm", step))
        step *= 2
    reduced = current
    factor_one = rounded_dot(strip[:, :w], first_inverse)
    next_panel = reduced_by(strip[:, w : 2 * w], factor_one, one_next)
    factor_two = rounded_dot(next_panel, second_inverse)
    far_one, far_two = jnp.split(far, 2, 1)
    second_far = reduced_by(far_two, factor_at_two, far_one)
    one_rows = jnp.concatenate([one_edge, far_one], 1)
    two_rows = jnp.concatenate([second_edge, second_far], 1)
    updated = reduced_by(strip[:, 2 * w :], factor_one, one_rows)
    trailing = reduced_by(updated, factor_two, two_rows)
    return (trailing[None], reduced[None])


def solution(mesh):
    placed = (P("tm", "blk", None), P("tm", None, None, None), P("tm", None, None), P())
    return jax.shard_map(
        body,
        mesh=mesh,
        in_specs=placed,
        out_specs=(P("tm", "blk", None), P("tm", None, None)),
        check_vma=False,
    )
```

profile of v0, /device:TPU:40, one launch (start us, length us, event | category | flops | bytes accessed | tf_op | source)
XLA Modules:
  0.0 128.9 jit_solution(8305294757422915728)
XLA Ops:
  7.2 0.0 copy-start.1
  7.2 0.0 all-gather.2.cloned.1.call-start
  7.2 0.8 dynamic-slice_subtract_fusion
  8.0 0.1 eq.10
  8.1 2.2 %convolution_convert_fusion = bf16[48,2304]{1,0:T(8,128)(2,1)S(1)} fusion(s32[48]{0:T(128)S(1)} %eq.10, bf16[1,512,2304]{2,1,0:T(8,128)(2,1)} %param.4), kind=kOutput, calls=%fused_computation.2 | convolution fusion | flops 113381376 | bytes 2580672 | tf_op jit(solution)/shard_map/dot_general | solution.py:17
  10.3 0.6 pad_maximum_fusion
  11.0 0.0 all-gather.2.cloned.1.call-update
  11.0 0.0 copy-done.1
  11.0 3.4 %collective-permute-start = (f32[256,256]{1,0:T(8,128)S(1)}, f32[256,256]{1,0:T(8,128)}, u32[]{:S(2)}, u32[]{:S(2)}) collective-permute-start(f32[256,256]{1,0:T(8,128)S(1)} %bitcast.64), channel_id=1, source_target_pairs={{0,16},{16,32},{32,48},{48,64},{64,80},{80,96},{96,112},{112,128},... | collective-permute-start | bytes 786440 | tf_op jit(solution)/shard_map/ppermute | solution.py:9
  14.5 0.0 copy-start
  14.5 26.1 %all_gather.6 = bf16[256,1792]{1,0:T(8,128)(2,1)S(1)} all-gather(bf16[16,1792]{1,0:T(8,128)(2,1)S(1)} %pad_maximum_fusion.1), channel_id=1, replica_groups=mesh['tm'=32,'blk'=16] {'blk'}, dimensions={0}, use_global_device_ids=true | all-gather | bytes 974848 | tf_op jit(solution)/shard_map/all_gather | solution.py:44
  40.6 1.9 %convolution_convert_fusion.5 = bf16[256,256]{1,0:T(8,128)(2,1)} fusion(bf16[256,1792]{1,0:T(8,128)(2,1)S(1)} %all_gather.6, bf16[1,2,256,256]{3,2,1,0:T(8,128)(2,1)} %param.5), kind=kOutput, calls=%fused_computation.24 | convolution fusion | flops 33619968 | bytes 393216 | tf_op jit(solution)/shard_map/dot_general | solution.py:17
  42.5 2.0 %fusion.3 = bf16[256,512]{1,0:T(8,128)(2,1)} fusion(bf16[256,1792]{1,0:T(8,128)(2,1)S(1)} %all_gather.6, bf16[1,2,256,256]{3,2,1,0:T(8,128)(2,1)} %param.5), kind=kOutput, calls=%fused_computation.11 | convolution fusion | flops 101122048 | bytes 1048576 | tf_op jit(solution)/shard_map/dot_general | solution.py:21
  44.4 1.7 %fusion.5 = bf16[256,256]{1,0:T(8,128)(2,1)} fusion(bf16[256,256]{1,0:T(8,128)(2,1)} %convolution_convert_fusion.5, bf16[256,1792]{1,0:T(8,128)(2,1)S(1)} %all_gather.6), kind=kOutput, calls=%fused_computation.20 | convolution fusion | flops 33751040 | bytes 524288 | tf_op jit(solution)/shard_map/dot_general | solution.py:21
  46.2 2.1 %fusion.6 = bf16[256,256]{1,0:T(8,128)(2,1)} fusion(bf16[256,256]{1,0:T(8,128)(2,1)} %fusion.5, bf16[256,512]{1,0:T(8,128)(2,1)} %fusion.3, bf16[1,2,256,256]{3,2,1,0:T(8,128)(2,1)} %param.5), kind=kOutput, calls=%fused_computation.21 | convolution fusion | flops 67371008 | bytes 655360 | tf_op jit(solution)/shard_map/dot_general | solution.py:21
  48.3 3.5 %collective-permute-start.4 = (bf16[256,256]{1,0:T(8,128)(2,1)}, bf16[256,256]{1,0:T(8,128)(2,1)}, u32[]{:S(2)}, u32[]{:S(2)}) collective-permute-start(bf16[256,256]{1,0:T(8,128)(2,1)} %fusion.6), channel_id=1, source_target_pairs={{0,16},{16,32},{32,48},{48,64},{64,80},{80,96},{96,112},{112,128},... | collective-permute-start | bytes 393224 | tf_op jit(solution)/shard_map/ppermute | solution.py:9
  51.8 0.0 copy-done
  51.8 1.8 %convolution_convert_fusion.2 = bf16[512,256]{1,0:T(8,128)(2,1)} fusion(bf16[512,2304]{1,0:T(8,128)(2,1)S(1)} %bitcast.61, bf16[1,2,256,256]{3,2,1,0:T(8,128)(2,1)} %param.5), kind=kOutput, calls=%fused_computation.9 | convolution fusion | flops 67239936 | bytes 655360 | tf_op jit(solution)/shard_map/dot_general | solution.py:17
  53.6 2.1 %convolution_convert_fusion.1 = bf16[512,256]{1,0:T(8,128)(2,1)} fusion(bf16[512,256]{1,0:T(8,128)(2,1)} %convolution_convert_fusion.2, bf16[512,2304]{1,0:T(8,128)(2,1)S(1)} %bitcast.62, bf16[256,1792]{1,0:T(8,128)(2,1)S(1)} %all_gather.6, bf16[1,2,256,256]{3,2,1,0:T(8,128)(2,1)} %param.5), kind=kOutput, calls=%fused_computation.8 | convolution fusion | flops 134742016 | bytes 1048576 | tf_op jit(solution)/shard_map/dot_general | solution.py:17
  55.7 0.0 copy-done.2
  55.7 2.7 %collective-permute-done.4 = bf16[256,256]{1,0:T(8,128)(2,1)} collective-permute-done((bf16[256,256]{1,0:T(8,128)(2,1)}, bf16[256,256]{1,0:T(8,128)(2,1)}, u32[]{:S(2)}, u32[]{:S(2)}) %collective-permute-start.4) | collective-permute-done | bytes 131104 | tf_op jit(solution)/shard_map/ppermute | solution.py:9
  58.3 1.2 fusion.42
  59.6 1.5 %fusion.51 = (bf16[256,256]{1,0:T(8,128)(2,1)S(1)}, f32[256,256]{1,0:T(8,128)S(1)}) fusion(bf16[256,256]{1,0:T(8,128)(2,1)} %fusion.6, f32[256,256]{1,0:T(8,128)S(1)} %fusion.42, f32[1,256,256]{2,1,0:T(8,128)S(1)} %copy-done.1), kind=kOutput, calls=%fused_computation.66 | convolution fusion | flops 201523200 | bytes 1048576 | tf_op jit(solution)/shard_map/dot_general | solution.py:13
  61.1 2.6 %collective-permute-start.5 = (bf16[256,256]{1,0:T(8,128)(2,1)S(1)}, bf16[256,256]{1,0:T(8,128)(2,1)S(1)}, u32[]{:S(2)}, u32[]{:S(2)}) collective-permute-start(bf16[256,256]{1,0:T(8,128)(2,1)S(1)} %get-tuple-element.6), channel_id=1, source_target_pairs={{0,32},{16,48},{32,64},{48,80},{64,96},{80,112},{96,128},{112,144}... | collective-permute-start | bytes 393224 | tf_op jit(solution)/shard_map/ppermute | solution.py:9
  63.7 0.0 collective-permute-done
  63.7 1.3 %fusion.44 = f32[256,256]{1,0:T(8,128)S(1)} fusion(f32[256,256]{1,0:T(8,128)} %collective-permute-done, f32[1,256,256]{2,1,0:T(8,128)S(1)} %copy-done.1), kind=kOutput, calls=%fused_computation.59 | convolution fusion | flops 201326592 | bytes 786432 | tf_op jit(solution)/shard_map/dot_general | solution.py:13
  65.0 4.7 %collective-permute-start.1 = (f32[256,256]{1,0:T(8,128)S(1)}, f32[256,256]{1,0:T(8,128)S(1)}, u32[]{:S(2)}, u32[]{:S(2)}) collective-permute-start(f32[256,256]{1,0:T(8,128)S(1)} %fusion.44), channel_id=1, source_target_pairs={{0,32},{16,48},{32,64},{48,80},{64,96},{80,112},{96,128},{112,144}... | collective-permute-start | bytes 786440 | tf_op jit(solution)/shard_map/ppermute | solution.py:9
  69.7 0.6 collective-permute-done.5
  70.4 0.3 fusion.58
  70.6 0.4 fusion.52
  71.0 2.4 %collective-permute-start.6 = (bf16[256,256]{1,0:T(8,128)(2,1)S(1)}, bf16[256,256]{1,0:T(8,128)(2,1)S(1)}, u32[]{:S(2)}, u32[]{:S(2)}) collective-permute-start(bf16[256,256]{1,0:T(8,128)(2,1)S(1)} %get-tuple-element.8), channel_id=1, source_target_pairs={{0,64},{16,80},{32,96},{48,112},{64,128},{80,144},{96,160},{112,17... | collective-permute-start | bytes 393224 | tf_op jit(solution)/shard_map/ppermute | solution.py:9
  73.5 4.7 %collective-permute-done.1 = f32[256,256]{1,0:T(8,128)S(1)} collective-permute-done((f32[256,256]{1,0:T(8,128)S(1)}, f32[256,256]{1,0:T(8,128)S(1)}, u32[]{:S(2)}, u32[]{:S(2)}) %collective-permute-start.1) | collective-permute-done | bytes 262176 | tf_op jit(solution)/shard_map/ppermute | solution.py:9
  78.2 0.4 fusion.55
  78.6 2.7 %collective-permute-start.2 = (f32[256,256]{1,0:T(8,128)S(1)}, f32[256,256]{1,0:T(8,128)S(1)}, u32[]{:S(2)}, u32[]{:S(2)}) collective-permute-start(f32[256,256]{1,0:T(8,128)S(1)} %fusion.55), channel_id=1, source_target_pairs={{0,64},{16,80},{32,96},{48,112},{64,128},{80,144},{96,160},{112,17... | collective-permute-start | bytes 786440 | tf_op jit(solution)/shard_map/ppermute | solution.py:9
  81.3 0.0 collective-permute-done.6
  81.3 0.3 fusion.59
  81.5 0.4 fusion.53
  82.0 1.9 %collective-permute-start.7 = (bf16[256,256]{1,0:T(8,128)(2,1)S(1)}, bf16[256,256]{1,0:T(8,128)(2,1)S(1)}, u32[]{:S(2)}, u32[]{:S(2)}) collective-permute-start(bf16[256,256]{1,0:T(8,128)(2,1)S(1)} %get-tuple-element.10), channel_id=1, source_target_pairs={{0,128},{16,144},{32,160},{48,176},{64,192},{80,208},{96,224},{112... | collective-permute-start | bytes 393224 | tf_op jit(solution)/shard_map/ppermute | solution.py:9
  83.9 6.6 %collective-permute-done.2 = f32[256,256]{1,0:T(8,128)S(1)} collective-permute-done((f32[256,256]{1,0:T(8,128)S(1)}, f32[256,256]{1,0:T(8,128)S(1)}, u32[]{:S(2)}, u32[]{:S(2)}) %collective-permute-start.2) | collective-permute-done | bytes 262176 | tf_op jit(solution)/shard_map/ppermute | solution.py:9
  90.4 0.4 fusion.56
  90.8 1.9 %collective-permute-start.3 = (f32[256,256]{1,0:T(8,128)S(1)}, f32[256,256]{1,0:T(8,128)S(1)}, u32[]{:S(2)}, u32[]{:S(2)}) collective-permute-start(f32[256,256]{1,0:T(8,128)S(1)} %fusion.56), channel_id=1, source_target_pairs={{0,128},{16,144},{32,160},{48,176},{64,192},{80,208},{96,224},{112... | collective-permute-start | bytes 786440 | tf_op jit(solution)/shard_map/ppermute | solution.py:9
  92.8 11.0 %collective-permute-done.7 = bf16[256,256]{1,0:T(8,128)(2,1)S(1)} collective-permute-done((bf16[256,256]{1,0:T(8,128)(2,1)S(1)}, bf16[256,256]{1,0:T(8,128)(2,1)S(1)}, u32[]{:S(2)}, u32[]{:S(2)}) %collective-permute-start.7) | collective-permute-done | bytes 131104 | tf_op jit(solution)/shard_map/ppermute | solution.py:9
  103.7 0.3 fusion.60
  104.0 0.4 fusion.54
  104.4 1.3 %collective-permute-start.8 = (bf16[256,256]{1,0:T(8,128)(2,1)S(1)}, bf16[256,256]{1,0:T(8,128)(2,1)S(1)}, u32[]{:S(2)}, u32[]{:S(2)}) collective-permute-start(bf16[256,256]{1,0:T(8,128)(2,1)S(1)} %get-tuple-element.12), channel_id=1, source_target_pairs={{0,256},{16,272},{32,288},{48,304},{64,320},{80,336},{96,352},{112... | collective-permute-start | bytes 393224 | tf_op jit(solution)/shard_map/ppermute | solution.py:9
  105.7 1.3 collective-permute-done.3
  107.0 0.4 fusion.57
  107.4 0.0 slice-start
  107.4 0.0 copy-start.5
  107.4 7.8 %collective-permute-done.8 = bf16[256,256]{1,0:T(8,128)(2,1)S(1)} collective-permute-done((bf16[256,256]{1,0:T(8,128)(2,1)S(1)}, bf16[256,256]{1,0:T(8,128)(2,1)S(1)}, u32[]{:S(2)}, u32[]{:S(2)}) %collective-permute-start.8) | collective-permute-done | bytes 131104 | tf_op jit(solution)/shard_map/ppermute | solution.py:9
  115.2 0.3 fusion.61
  115.5 1.1 fusion.4
  116.6 1.2 split.8
  117.8 0.0 slice-done
  117.8 0.0 copy-done.5
  117.8 0.0 copy-start.3
  117.8 0.0 copy-start.6
  117.8 0.6 subtract_convert_fusion.1
  118.4 0.7 copy-done.3
  119.2 0.0 copy-done.6
  119.2 0.4 fusion.1
  119.6 0.6 copy-done.4
  120.1 0.0 copy-done.7
  120.2 1.9 %fusion = bf16[1,512,1792]{2,1,0:T(8,128)(2,1)} fusion(bf16[512,256]{1,0:T(8,128)(2,1)S(1)} %copy-done.4, bf16[512,1792]{1,0:T(8,128)(2,1)S(1)} %subtract_convert_fusion.1, bf16[256,1536]{1,0:T(8,128)(2,1)S(1)} %fusion.1, bf16[256,256]{1,0:T(8,128)(2,1)S(1)} %copy-done.7), kind=kOutput, calls=%fused_computation.4 | convolution fusion | flops 474349568 | bytes 4849664 | tf_op jit(solution)/shard_map/dot_general | solution.py:21
  (9 shorter events, 0.0 us)
Async XLA Ops:
  7.2 3.8 %copy-start.1 = (f32[1,256,256]{2,1,0:T(8,128)S(1)}, f32[1,256,256]{2,1,0:T(8,128)}, u32[]{:S(2)}) copy-start(f32[1,256,256]{2,1,0:T(8,128)} %param.6) | copy-start | bytes 786436
  7.2 109.4 %all-gather.2.cloned.1.call-start = ((), (), s32[]{:S(2)}) async-start(), calls=%async_computation | async-start | bytes 1671168 | tf_op jit(solution)/shard_map/all_gather | solution.py:58
  11.0 52.7 %collective-permute-start = (f32[256,256]{1,0:T(8,128)S(1)}, f32[256,256]{1,0:T(8,128)}, u32[]{:S(2)}, u32[]{:S(2)}) collective-permute-start(f32[256,256]{1,0:T(8,128)S(1)} %bitcast.64), channel_id=1, source_target_pairs={{0,16},{16,32},{32,48},{48,64},{64,80},{80,96},{96,112},{112,128},... | collective-permute-start | bytes 786440 | tf_op jit(solution)/shard_map/ppermute | solution.py:9
  14.5 37.3 %copy-start = (bf16[1,512,2304]{2,1,0:T(8,128)(2,1)S(1)}, bf16[1,512,2304]{2,1,0:T(8,128)(2,1)}, u32[]{:S(2)}) copy-start(bf16[1,512,2304]{2,1,0:T(8,128)(2,1)} %param.4) | copy-start | bytes 7077892
  40.6 15.1 %copy-start.2 = (bf16[256,1792]{1,0:T(8,128)(2,1)}, bf16[256,1792]{1,0:T(8,128)(2,1)S(1)}, u32[]{:S(2)}) copy-start(bf16[256,1792]{1,0:T(8,128)(2,1)S(1)} %all_gather.6) | copy-start | bytes 2752516
  48.3 10.1 %collective-permute-start.4 = (bf16[256,256]{1,0:T(8,128)(2,1)}, bf16[256,256]{1,0:T(8,128)(2,1)}, u32[]{:S(2)}, u32[]{:S(2)}) collective-permute-start(bf16[256,256]{1,0:T(8,128)(2,1)} %fusion.6), channel_id=1, source_target_pairs={{0,16},{16,32},{32,48},{48,64},{64,80},{80,96},{96,112},{112,128},... | collective-permute-start | bytes 393224 | tf_op jit(solution)/shard_map/ppermute | solution.py:9
  61.1 9.3 %collective-permute-start.5 = (bf16[256,256]{1,0:T(8,128)(2,1)S(1)}, bf16[256,256]{1,0:T(8,128)(2,1)S(1)}, u32[]{:S(2)}, u32[]{:S(2)}) collective-permute-start(bf16[256,256]{1,0:T(8,128)(2,1)S(1)} %get-tuple-element.6), channel_id=1, source_target_pairs={{0,32},{16,48},{32,64},{48,80},{64,96},{80,112},{96,128},{112,144}... | collective-permute-start | bytes 393224 | tf_op jit(solution)/shard_map/ppermute | solution.py:9
  65.0 13.2 %collective-permute-start.1 = (f32[256,256]{1,0:T(8,128)S(1)}, f32[256,256]{1,0:T(8,128)S(1)}, u32[]{:S(2)}, u32[]{:S(2)}) collective-permute-start(f32[256,256]{1,0:T(8,128)S(1)} %fusion.44), channel_id=1, source_target_pairs={{0,32},{16,48},{32,64},{48,80},{64,96},{80,112},{96,128},{112,144}... | collective-permute-start | bytes 786440 | tf_op jit(solution)/shard_map/ppermute | solution.py:9
  71.0 10.2 %collective-permute-start.6 = (bf16[256,256]{1,0:T(8,128)(2,1)S(1)}, bf16[256,256]{1,0:T(8,128)(2,1)S(1)}, u32[]{:S(2)}, u32[]{:S(2)}) collective-permute-start(bf16[256,256]{1,0:T(8,128)(2,1)S(1)} %get-tuple-element.8), channel_id=1, source_target_pairs={{0,64},{16,80},{32,96},{48,112},{64,128},{80,144},{96,160},{112,17... | collective-permute-start | bytes 393224 | tf_op jit(solution)/shard_map/ppermute | solution.py:9
  78.6 11.8 %collective-permute-start.2 = (f32[256,256]{1,0:T(8,128)S(1)}, f32[256,256]{1,0:T(8,128)S(1)}, u32[]{:S(2)}, u32[]{:S(2)}) collective-permute-start(f32[256,256]{1,0:T(8,128)S(1)} %fusion.55), channel_id=1, source_target_pairs={{0,64},{16,80},{32,96},{48,112},{64,128},{80,144},{96,160},{112,17... | collective-permute-start | bytes 786440 | tf_op jit(solution)/shard_map/ppermute | solution.py:9
  82.0 21.7 %collective-permute-start.7 = (bf16[256,256]{1,0:T(8,128)(2,1)S(1)}, bf16[256,256]{1,0:T(8,128)(2,1)S(1)}, u32[]{:S(2)}, u32[]{:S(2)}) collective-permute-start(bf16[256,256]{1,0:T(8,128)(2,1)S(1)} %get-tuple-element.10), channel_id=1, source_target_pairs={{0,128},{16,144},{32,160},{48,176},{64,192},{80,208},{96,224},{112... | collective-permute-start | bytes 393224 | tf_op jit(solution)/shard_map/ppermute | solution.py:9
  90.8 16.1 %collective-permute-start.3 = (f32[256,256]{1,0:T(8,128)S(1)}, f32[256,256]{1,0:T(8,128)S(1)}, u32[]{:S(2)}, u32[]{:S(2)}) collective-permute-start(f32[256,256]{1,0:T(8,128)S(1)} %fusion.56), channel_id=1, source_target_pairs={{0,128},{16,144},{32,160},{48,176},{64,192},{80,208},{96,224},{112... | collective-permute-start | bytes 786440 | tf_op jit(solution)/shard_map/ppermute | solution.py:9
  104.4 10.8 %collective-permute-start.8 = (bf16[256,256]{1,0:T(8,128)(2,1)S(1)}, bf16[256,256]{1,0:T(8,128)(2,1)S(1)}, u32[]{:S(2)}, u32[]{:S(2)}) collective-permute-start(bf16[256,256]{1,0:T(8,128)(2,1)S(1)} %get-tuple-element.12), channel_id=1, source_target_pairs={{0,256},{16,272},{32,288},{48,304},{64,320},{80,336},{96,352},{112... | collective-permute-start | bytes 393224 | tf_op jit(solution)/shard_map/ppermute | solution.py:9
  107.4 10.4 %slice-start = ((bf16[256,1792]{1,0:T(8,128)(2,1)}), bf16[256,256]{1,0:T(8,128)(2,1)S(1)}, s32[]{:S(2)}) async-start(bf16[256,1792]{1,0:T(8,128)(2,1)} %copy-done.2), calls=%async_computation.1 | async-start | bytes 262144 | tf_op jit(solution)/shard_map/slice | solution.py:61
  107.4 10.4 %copy-start.5 = (bf16[512,256]{1,0:T(8,128)(2,1)S(1)}, bf16[512,256]{1,0:T(8,128)(2,1)}, u32[]{:S(2)}) copy-start(bf16[512,256]{1,0:T(8,128)(2,1)} %convolution_convert_fusion.2) | copy-start | bytes 786436
  117.8 1.4 %copy-start.3 = (bf16[256,3072]{1,0:T(8,128)(2,1)S(1)}, bf16[256,3072]{1,0:T(8,128)(2,1)}, u32[]{:S(2)}) copy-start(bf16[256,3072]{1,0:T(8,128)(2,1)} %all-gather.2.cloned.1.call-done) | copy-start | bytes 4718596
  117.8 1.4 %copy-start.6 = (bf16[256,256]{1,0:T(8,128)(2,1)S(1)}, bf16[256,256]{1,0:T(8,128)(2,1)}, u32[]{:S(2)}) copy-start(bf16[256,256]{1,0:T(8,128)(2,1)} %convolution_convert_fusion.5) | copy-start | bytes 393220
  119.2 1.0 copy-start.4
  119.2 1.0 copy-start.7
Sparse Core Ops, SparseCore 0:
  11.1 46.6 all-gather.1
where the time goes:
time: 130 us; the launch traced here: 129 us
  waiting for transfers between devices  34.6 us (27%)
  blocking collectives  26.1 us (20%)
  matrix products  25.3 us (19%)
  starting transfers between devices  24.4 us (19%)
  between operations  14.4 us (11%)
  local copies, waits for them, and re-layouts  2.66 us (2%)
  other arithmetic  1.44 us (1%)
    ppermute x9, waiting for transfers between devices, passed_along(): return lax.ppermute(x, axis, [(i, i + by) for i in range(count - by)])  34.6 us
    all_gather x1, blocking collectives, body(): lax.all_gather(jnp.concatenate([rows_one[:, w:3 * w], rows_two[:, :w], ro...  26.1 us
    ppermute x9, starting transfers between devices, passed_along(): return lax.ppermute(x, axis, [(i, i + by) for i in range(count - by)])  24.4 us
    dot_general x6, matrix products, reduced_by(): product = jnp.dot(factor, rows, preferred_element_type=jnp.float32)  8.68 us
    dot_general x14, matrix products, matmul_high(): jnp.dot(left, right, precision=lax.Precision.HIGHEST, preferred_element_t...  8.61 us
    dot_general x4, matrix products, rounded_dot(): jnp.dot(left, right, preferred_element_type=jnp.float32)  7.99 us
  transfers between devices with their start and end apart: 10, of which 7 were waited for; matrix products, arithmetic and copies ran while one was open for 16% of the time, Pallas kernels for 0%

commit v1 on v0

--- a/solution.py
+++ b/solution.py
@@ -41,19 +41,27 @@
     rows_one, rows_two, rows_edge = (
         picked[i * per_device : (i + 1) * per_device] for i in range(3)
     )
-    near = lax.all_gather(
-        jnp.concatenate(
-            [
-                rows_one[:, w : 3 * w],
-                rows_two[:, :w],
-                rows_two[:, 2 * w : 3 * w],
-                rows_edge[:, : 3 * w],
-            ],
-            1,
+    near = jnp.concatenate(
+        lax.all_to_all(
+            jnp.stack(
+                [
+                    jnp.concatenate(
+                        [
+                            rows_one[:, w : 3 * w],
+                            rows_two[:, :w],
+                            rows_two[:, 2 * w : 3 * w],
+                            rows_edge[:, : 3 * w],
+                        ],
+                        1,
+                    )
+                ]
+                * lax.axis_size("blk")
+            ),
+            "blk",
+            0,
+            0,
         ),
-        "blk",
         axis=0,
-        tiled=True,
     )
     far = lax.all_gather(
         jnp.concatenate([rows_one[:, 3 * w :], rows_two[:, 3 * w :]], 1), "blk", axis=0, tiled=True

time: 130 us -> 137 us (1.054)
  the two profiles are of different devices: /device:TPU:40 before, /device:TPU:32 now
where the time goes in v1:
time: 137 us; the launch traced here: 136 us
  waiting for transfers between devices  55.1 us (40%)
  starting transfers between devices  33 us (24%)
  matrix products  28.1 us (21%)
  between operations  14.4 us (11%)
  local copies, waits for them, and re-layouts  4.37 us (3%)
  other arithmetic  1.4 us (1%)
    ppermute x9, waiting for transfers between devices, passed_along(): return lax.ppermute(x, axis, [(i, i + by) for i in range(count - by)])  37.8 us
    ppermute x9, starting transfers between devices, passed_along(): return lax.ppermute(x, axis, [(i, i + by) for i in range(count - by)])  22.4 us
    all_to_all x1, waiting for transfers between devices, body(): lax.all_to_all(jnp.stack([jnp.concatenate([rows_one[:, w:3 * w], rows_two...  17.3 us
    all_to_all x1, starting transfers between devices, body(): lax.all_to_all(jnp.stack([jnp.concatenate([rows_one[:, w:3 * w], rows_two...  10.6 us
    dot_general x14, matrix products, matmul_high(): jnp.dot(left, right, precision=lax.Precision.HIGHEST, preferred_element_t...  10.3 us
    dot_general x6, matrix products, reduced_by(): product = jnp.dot(factor, rows, preferred_element_type=jnp.float32)  9.82 us
    dot_general x4, matrix products, rounded_dot(): jnp.dot(left, right, preferred_element_type=jnp.float32)  7.92 us
  transfers between devices with their start and end apart: 11, of which 8 were waited for; matrix products, arithmetic and copies ran while one was open for 18% of the time, Pallas kernels for 0%

profile of v1, /device:TPU:32, one launch (start us, length us, event | category | flops | bytes accessed | tf_op | source)
XLA Modules:
  0.0 136.3 jit_solution(8794957937398210629)
XLA Ops:
  7.2 0.8 dynamic-slice_subtract_fusion
  7.9 0.1 eq.10
  8.0 2.2 %convolution_convert_fusion = bf16[48,2304]{1,0:T(8,128)(2,1)S(1)} fusion(s32[48]{0:T(128)S(1)} %eq.10, bf16[1,512,2304]{2,1,0:T(8,128)(2,1)} %param.4), kind=kOutput, calls=%fused_computation.2 | convolution fusion | flops 113381376 | bytes 2580672 | tf_op jit(solution)/shard_map/dot_general | solution.py:17
  10.2 0.0 copy-start.2
  10.3 0.0 copy-start.1
  10.3 0.0 copy-start
  10.3 1.0 stack.2
  11.3 0.0 copy-done.2
  11.3 10.6 %all-to-all-start = ((bf16[16,16,1792]{2,1,0:T(8,128)(2,1)}), bf16[16,16,1792]{2,1,0:T(8,128)(2,1)S(1)}, u32[]{:S(2)}, u32[]{:S(2)}) async-start(bf16[16,16,1792]{2,1,0:T(8,128)(2,1)} %stack.2), calls=%async_computation | async-start | bytes 1835008 | tf_op jit(solution)/shard_map/all_to_all | solution.py:45
  21.9 0.0 all-gather.2.cloned.1.call-start
  21.9 0.8 fusion.49
  22.8 0.6 pad_maximum_fusion
  23.4 0.0 all-gather.2.cloned.1.call-update
  23.4 0.0 copy-done.1
  23.4 3.4 %collective-permute-start = (f32[256,256]{1,0:T(8,128)S(1)}, f32[256,256]{1,0:T(8,128)}, u32[]{:S(2)}, u32[]{:S(2)}) collective-permute-start(f32[256,256]{1,0:T(8,128)S(1)} %bitcast.65), channel_id=1, source_target_pairs={{0,16},{16,32},{32,48},{48,64},{64,80},{80,96},{96,112},{112,128},... | collective-permute-start | bytes 786440 | tf_op jit(solution)/shard_map/ppermute | solution.py:9
  26.8 0.0 copy-done
  26.8 1.9 %convolution_convert_fusion.2 = bf16[512,256]{1,0:T(8,128)(2,1)} fusion(bf16[512,2304]{1,0:T(8,128)(2,1)S(1)} %bitcast.62, bf16[1,2,256,256]{3,2,1,0:T(8,128)(2,1)} %param.5), kind=kOutput, calls=%fused_computation.9 | convolution fusion | flops 67239936 | bytes 655360 | tf_op jit(solution)/shard_map/dot_general | solution.py:17
  28.7 17.3 %all-to-all-done = bf16[16,16,1792]{2,1,0:T(8,128)(2,1)S(1)} async-done(((bf16[16,16,1792]{2,1,0:T(8,128)(2,1)}), bf16[16,16,1792]{2,1,0:T(8,128)(2,1)S(1)}, u32[]{:S(2)}, u32[]{:S(2)}) %all-to-all-start) | async-done | bytes 917536 | tf_op jit(solution)/shard_map/all_to_all | solution.py:45
  46.0 1.7 %convolution_convert_fusion.5 = bf16[256,256]{1,0:T(8,128)(2,1)} fusion(bf16[256,1792]{1,0:T(8,128)(2,1)S(1)} %bitcast.66, bf16[1,2,256,256]{3,2,1,0:T(8,128)(2,1)} %param.5), kind=kOutput, calls=%fused_computation.24 | convolution fusion | flops 33619968 | bytes 393216 | tf_op jit(solution)/shard_map/dot_general | solution.py:17
  47.7 2.0 %fusion.3 = bf16[256,512]{1,0:T(8,128)(2,1)} fusion(bf16[256,1792]{1,0:T(8,128)(2,1)S(1)} %bitcast.67, bf16[1,2,256,256]{3,2,1,0:T(8,128)(2,1)} %param.5), kind=kOutput, calls=%fused_computation.11 | convolution fusion | flops 101122048 | bytes 1048576 | tf_op jit(solution)/shard_map/dot_general | solution.py:21
  49.7 1.8 %fusion.5 = bf16[256,256]{1,0:T(8,128)(2,1)} fusion(bf16[256,256]{1,0:T(8,128)(2,1)} %convolution_convert_fusion.5, bf16[256,1792]{1,0:T(8,128)(2,1)S(1)} %bitcast.68), kind=kOutput, calls=%fused_computation.20 | convolution fusion | flops 33751040 | bytes 524288 | tf_op jit(solution)/shard_map/dot_general | solution.py:21
  51.4 2.1 %fusion.6 = bf16[256,256]{1,0:T(8,128)(2,1)} fusion(bf16[256,256]{1,0:T(8,128)(2,1)} %fusion.5, bf16[256,512]{1,0:T(8,128)(2,1)} %fusion.3, bf16[1,2,256,256]{3,2,1,0:T(8,128)(2,1)} %param.5), kind=kOutput, calls=%fused_computation.21 | convolution fusion | flops 67371008 | bytes 655360 | tf_op jit(solution)/shard_map/dot_general | solution.py:21
  53.5 3.4 %collective-permute-start.4 = (bf16[256,256]{1,0:T(8,128)(2,1)}, bf16[256,256]{1,0:T(8,128)(2,1)S(1)}, u32[]{:S(2)}, u32[]{:S(2)}) collective-permute-start(bf16[256,256]{1,0:T(8,128)(2,1)} %fusion.6), channel_id=1, source_target_pairs={{0,16},{16,32},{32,48},{48,64},{64,80},{80,96},{96,112},{112,128},... | collective-permute-start | bytes 393224 | tf_op jit(solution)/shard_map/ppermute | solution.py:9
  57.0 0.0 collective-permute-done
  57.0 1.3 fusion.44
  58.3 4.7 %collective-permute-start.1 = (f32[256,256]{1,0:T(8,128)S(1)}, f32[256,256]{1,0:T(8,128)S(1)}, u32[]{:S(2)}, u32[]{:S(2)}) collective-permute-start(f32[256,256]{1,0:T(8,128)S(1)} %fusion.44), channel_id=1, source_target_pairs={{0,32},{16,48},{32,64},{48,80},{64,96},{80,112},{96,128},{112,144}... | collective-permute-start | bytes 786440 | tf_op jit(solution)/shard_map/ppermute | solution.py:9
  63.0 2.0 %collective-permute-done.4 = bf16[256,256]{1,0:T(8,128)(2,1)S(1)} collective-permute-done((bf16[256,256]{1,0:T(8,128)(2,1)}, bf16[256,256]{1,0:T(8,128)(2,1)S(1)}, u32[]{:S(2)}, u32[]{:S(2)}) %collective-permute-start.4) | collective-permute-done | bytes 131104 | tf_op jit(solution)/shard_map/ppermute | solution.py:9
  65.0 0.3 fusion.42
  65.3 1.5 %fusion.51 = (bf16[256,256]{1,0:T(8,128)(2,1)S(1)}, f32[256,256]{1,0:T(8,128)S(1)}) fusion(bf16[256,256]{1,0:T(8,128)(2,1)} %fusion.6, f32[256,256]{1,0:T(8,128)S(1)} %fusion.42, f32[1,256,256]{2,1,0:T(8,128)S(1)} %copy-done.1), kind=kOutput, calls=%fused_computation.66 | convolution fusion | flops 201523200 | bytes 1048576 | tf_op jit(solution)/shard_map/dot_general | solution.py:13
  66.8 1.9 %collective-permute-start.5 = (bf16[256,256]{1,0:T(8,128)(2,1)S(1)}, bf16[256,256]{1,0:T(8,128)(2,1)S(1)}, u32[]{:S(2)}, u32[]{:S(2)}) collective-permute-start(bf16[256,256]{1,0:T(8,128)(2,1)S(1)} %get-tuple-element.6), channel_id=1, source_target_pairs={{0,32},{16,48},{32,64},{48,80},{64,96},{80,112},{96,128},{112,144}... | collective-permute-start | bytes 393224 | tf_op jit(solution)/shard_map/ppermute | solution.py:9
  68.8 4.2 %collective-permute-done.1 = f32[256,256]{1,0:T(8,128)S(1)} collective-permute-done((f32[256,256]{1,0:T(8,128)S(1)}, f32[256,256]{1,0:T(8,128)S(1)}, u32[]{:S(2)}, u32[]{:S(2)}) %collective-permute-start.1) | collective-permute-done | bytes 262176 | tf_op jit(solution)/shard_map/ppermute | solution.py:9
  73.0 0.4 fusion.55
  73.3 1.9 %collective-permute-start.2 = (f32[256,256]{1,0:T(8,128)S(1)}, f32[256,256]{1,0:T(8,128)S(1)}, u32[]{:S(2)}, u32[]{:S(2)}) collective-permute-start(f32[256,256]{1,0:T(8,128)S(1)} %fusion.55), channel_id=1, source_target_pairs={{0,64},{16,80},{32,96},{48,112},{64,128},{80,144},{96,160},{112,17... | collective-permute-start | bytes 786440 | tf_op jit(solution)/shard_map/ppermute | solution.py:9
  75.3 2.6 %collective-permute-done.5 = bf16[256,256]{1,0:T(8,128)(2,1)S(1)} collective-permute-done((bf16[256,256]{1,0:T(8,128)(2,1)S(1)}, bf16[256,256]{1,0:T(8,128)(2,1)S(1)}, u32[]{:S(2)}, u32[]{:S(2)}) %collective-permute-start.5) | collective-permute-done | bytes 131104 | tf_op jit(solution)/shard_map/ppermute | solution.py:9
  77.9 0.3 fusion.58
  78.2 0.4 fusion.52
  78.6 1.9 %collective-permute-start.6 = (bf16[256,256]{1,0:T(8,128)(2,1)S(1)}, bf16[256,256]{1,0:T(8,128)(2,1)S(1)}, u32[]{:S(2)}, u32[]{:S(2)}) collective-permute-start(bf16[256,256]{1,0:T(8,128)(2,1)S(1)} %get-tuple-element.8), channel_id=1, source_target_pairs={{0,64},{16,80},{32,96},{48,112},{64,128},{80,144},{96,160},{112,17... | collective-permute-start | bytes 393224 | tf_op jit(solution)/shard_map/ppermute | solution.py:9
  80.5 5.1 %collective-permute-done.2 = f32[256,256]{1,0:T(8,128)S(1)} collective-permute-done((f32[256,256]{1,0:T(8,128)S(1)}, f32[256,256]{1,0:T(8,128)S(1)}, u32[]{:S(2)}, u32[]{:S(2)}) %collective-permute-start.2) | collective-permute-done | bytes 262176 | tf_op jit(solution)/shard_map/ppermute | solution.py:9
  85.6 0.4 fusion.56
  86.0 1.9 %collective-permute-start.3 = (f32[256,256]{1,0:T(8,128)S(1)}, f32[256,256]{1,0:T(8,128)S(1)}, u32[]{:S(2)}, u32[]{:S(2)}) collective-permute-start(f32[256,256]{1,0:T(8,128)S(1)} %fusion.56), channel_id=1, source_target_pairs={{0,128},{16,144},{32,160},{48,176},{64,192},{80,208},{96,224},{112... | collective-permute-start | bytes 786440 | tf_op jit(solution)/shard_map/ppermute | solution.py:9
  87.9 0.0 collective-permute-done.6
  87.9 0.3 fusion.59
  88.2 0.4 fusion.53
  88.6 1.9 %collective-permute-start.7 = (bf16[256,256]{1,0:T(8,128)(2,1)S(1)}, bf16[256,256]{1,0:T(8,128)(2,1)S(1)}, u32[]{:S(2)}, u32[]{:S(2)}) collective-permute-start(bf16[256,256]{1,0:T(8,128)(2,1)S(1)} %get-tuple-element.10), channel_id=1, source_target_pairs={{0,128},{16,144},{32,160},{48,176},{64,192},{80,208},{96,224},{112... | collective-permute-start | bytes 393224 | tf_op jit(solution)/shard_map/ppermute | solution.py:9
  90.5 15.9 %collective-permute-done.3 = f32[256,256]{1,0:T(8,128)S(1)} collective-permute-done((f32[256,256]{1,0:T(8,128)S(1)}, f32[256,256]{1,0:T(8,128)S(1)}, u32[]{:S(2)}, u32[]{:S(2)}) %collective-permute-start.3) | collective-permute-done | bytes 262176 | tf_op jit(solution)/shard_map/ppermute | solution.py:9
  106.4 0.4 fusion.57
  106.8 0.7 slice.98
  107.5 0.4 collective-permute-done.7
  107.8 0.3 fusion.60
  108.1 1.2 fusion.54
  109.3 1.3 collective-permute-start.8
  110.6 2.1 %convolution_convert_fusion.1 = bf16[512,256]{1,0:T(8,128)(2,1)} fusion(bf16[512,256]{1,0:T(8,128)(2,1)} %convolution_convert_fusion.2, bf16[512,2304]{1,0:T(8,128)(2,1)S(1)} %bitcast.63, bf16[256,1792]{1,0:T(8,128)(2,1)S(1)} %bitcast.70, bf16[1,2,256,256]{3,2,1,0:T(8,128)(2,1)} %param.5), kind=kOutput, calls=%fused_computation.8 | convolution fusion | flops 134742016 | bytes 1048576 | tf_op jit(solution)/shard_map/dot_general | solution.py:17
  112.6 7.7 %collective-permute-done.8 = bf16[256,256]{1,0:T(8,128)(2,1)} collective-permute-done((bf16[256,256]{1,0:T(8,128)(2,1)}, bf16[256,256]{1,0:T(8,128)(2,1)}, u32[]{:S(2)}, u32[]{:S(2)}) %collective-permute-start.8) | collective-permute-done | bytes 131104 | tf_op jit(solution)/shard_map/ppermute | solution.py:9
  120.3 1.2 fusion.61
  121.5 2.1 %fusion.4 = f32[1,256,256]{2,1,0:T(8,128)} fusion(f32[256,256]{1,0:T(8,128)} %get-tuple-element.13, f32[256,256]{1,0:T(8,128)S(1)} %fusion.61, f32[256,256]{1,0:T(8,128)S(1)} %fusion.57), kind=kOutput, calls=%fused_computation.13 | convolution fusion | flops 201392128 | bytes 1048576 | tf_op jit(solution)/shard_map/dot_general | solution.py:13
  123.6 1.2 split.8
  124.8 0.0 copy-start.3
  124.8 0.0 copy-start.5
  124.8 1.7 %subtract_convert_fusion.1 = bf16[512,1792]{1,0:T(8,128)(2,1)S(1)} fusion(bf16[512,256]{1,0:T(8,128)(2,1)} %convolution_convert_fusion.2, bf16[512,2304]{1,0:T(8,128)(2,1)S(1)} %bitcast.64, bf16[256,1536]{1,0:T(8,128)(2,1)S(1)} %split.8, bf16[256,256]{1,0:T(8,128)(2,1)} %slice.98), kind=kOutput, calls=%fused_computation.1 | convolution fusion | flops 474349568 | bytes 4849664 | tf_op jit(solution)/shard_map/dot_general | solution.py:21
  126.6 0.0 copy-start.4
  126.6 0.4 fusion.1
  127.0 0.5 copy-done.4
  127.5 0.0 copy-done.6
  127.6 1.9 %fusion = bf16[1,512,1792]{2,1,0:T(8,128)(2,1)} fusion(bf16[512,256]{1,0:T(8,128)(2,1)S(1)} %copy-done.4, bf16[512,1792]{1,0:T(8,128)(2,1)S(1)} %subtract_convert_fusion.1, bf16[256,1536]{1,0:T(8,128)(2,1)S(1)} %fusion.1, bf16[256,256]{1,0:T(8,128)(2,1)S(1)} %copy-done.6), kind=kOutput, calls=%fused_computation.4 | convolution fusion | flops 474349568 | bytes 4849664 | tf_op jit(solution)/shard_map/dot_general | solution.py:21
  (8 shorter events, 0.0 us)
Async XLA Ops:
  10.2 1.1 copy-start.2
  10.3 13.2 %copy-start.1 = (f32[1,256,256]{2,1,0:T(8,128)S(1)}, f32[1,256,256]{2,1,0:T(8,128)}, u32[]{:S(2)}) copy-start(f32[1,256,256]{2,1,0:T(8,128)} %param.6) | copy-start | bytes 786436
  10.3 16.6 %copy-start = (bf16[1,512,2304]{2,1,0:T(8,128)(2,1)S(1)}, bf16[1,512,2304]{2,1,0:T(8,128)(2,1)}, u32[]{:S(2)}) copy-start(bf16[1,512,2304]{2,1,0:T(8,128)(2,1)} %param.4) | copy-start | bytes 7077892
  11.3 34.7 %all-to-all-start = ((bf16[16,16,1792]{2,1,0:T(8,128)(2,1)}), bf16[16,16,1792]{2,1,0:T(8,128)(2,1)S(1)}, u32[]{:S(2)}, u32[]{:S(2)}) async-start(bf16[16,16,1792]{2,1,0:T(8,128)(2,1)} %stack.2), calls=%async_computation | async-start | bytes 1835008 | tf_op jit(solution)/shard_map/all_to_all | solution.py:45
  21.9 101.7 %all-gather.2.cloned.1.call-start = ((), (), s32[]{:S(2)}) async-start(), calls=%async_computation.1 | async-start | bytes 1671168 | tf_op jit(solution)/shard_map/all_gather | solution.py:66
  23.4 33.5 %collective-permute-start = (f32[256,256]{1,0:T(8,128)S(1)}, f32[256,256]{1,0:T(8,128)}, u32[]{:S(2)}, u32[]{:S(2)}) collective-permute-start(f32[256,256]{1,0:T(8,128)S(1)} %bitcast.65), channel_id=1, source_target_pairs={{0,16},{16,32},{32,48},{48,64},{64,80},{80,96},{96,112},{112,128},... | collective-permute-start | bytes 786440 | tf_op jit(solution)/shard_map/ppermute | solution.py:9
  53.5 11.5 %collective-permute-start.4 = (bf16[256,256]{1,0:T(8,128)(2,1)}, bf16[256,256]{1,0:T(8,128)(2,1)S(1)}, u32[]{:S(2)}, u32[]{:S(2)}) collective-permute-start(bf16[256,256]{1,0:T(8,128)(2,1)} %fusion.6), channel_id=1, source_target_pairs={{0,16},{16,32},{32,48},{48,64},{64,80},{80,96},{96,112},{112,128},... | collective-permute-start | bytes 393224 | tf_op jit(solution)/shard_map/ppermute | solution.py:9
  58.3 14.7 %collective-permute-start.1 = (f32[256,256]{1,0:T(8,128)S(1)}, f32[256,256]{1,0:T(8,128)S(1)}, u32[]{:S(2)}, u32[]{:S(2)}) collective-permute-start(f32[256,256]{1,0:T(8,128)S(1)} %fusion.44), channel_id=1, source_target_pairs={{0,32},{16,48},{32,64},{48,80},{64,96},{80,112},{96,128},{112,144}... | collective-permute-start | bytes 786440 | tf_op jit(solution)/shard_map/ppermute | solution.py:9
  66.8 11.0 %collective-permute-start.5 = (bf16[256,256]{1,0:T(8,128)(2,1)S(1)}, bf16[256,256]{1,0:T(8,128)(2,1)S(1)}, u32[]{:S(2)}, u32[]{:S(2)}) collective-permute-start(bf16[256,256]{1,0:T(8,128)(2,1)S(1)} %get-tuple-element.6), channel_id=1, source_target_pairs={{0,32},{16,48},{32,64},{48,80},{64,96},{80,112},{96,128},{112,144}... | collective-permute-start | bytes 393224 | tf_op jit(solution)/shard_map/ppermute | solution.py:9
  73.3 12.3 %collective-permute-start.2 = (f32[256,256]{1,0:T(8,128)S(1)}, f32[256,256]{1,0:T(8,128)S(1)}, u32[]{:S(2)}, u32[]{:S(2)}) collective-permute-start(f32[256,256]{1,0:T(8,128)S(1)} %fusion.55), channel_id=1, source_target_pairs={{0,64},{16,80},{32,96},{48,112},{64,128},{80,144},{96,160},{112,17... | collective-permute-start | bytes 786440 | tf_op jit(solution)/shard_map/ppermute | solution.py:9
  78.6 9.3 %collective-permute-start.6 = (bf16[256,256]{1,0:T(8,128)(2,1)S(1)}, bf16[256,256]{1,0:T(8,128)(2,1)S(1)}, u32[]{:S(2)}, u32[]{:S(2)}) collective-permute-start(bf16[256,256]{1,0:T(8,128)(2,1)S(1)} %get-tuple-element.8), channel_id=1, source_target_pairs={{0,64},{16,80},{32,96},{48,112},{64,128},{80,144},{96,160},{112,17... | collective-permute-start | bytes 393224 | tf_op jit(solution)/shard_map/ppermute | solution.py:9
  86.0 20.4 %collective-permute-start.3 = (f32[256,256]{1,0:T(8,128)S(1)}, f32[256,256]{1,0:T(8,128)S(1)}, u32[]{:S(2)}, u32[]{:S(2)}) collective-permute-start(f32[256,256]{1,0:T(8,128)S(1)} %fusion.56), channel_id=1, source_target_pairs={{0,128},{16,144},{32,160},{48,176},{64,192},{80,208},{96,224},{112... | collective-permute-start | bytes 786440 | tf_op jit(solution)/shard_map/ppermute | solution.py:9
  88.6 19.2 %collective-permute-start.7 = (bf16[256,256]{1,0:T(8,128)(2,1)S(1)}, bf16[256,256]{1,0:T(8,128)(2,1)S(1)}, u32[]{:S(2)}, u32[]{:S(2)}) collective-permute-start(bf16[256,256]{1,0:T(8,128)(2,1)S(1)} %get-tuple-element.10), channel_id=1, source_target_pairs={{0,128},{16,144},{32,160},{48,176},{64,192},{80,208},{96,224},{112... | collective-permute-start | bytes 393224 | tf_op jit(solution)/shard_map/ppermute | solution.py:9
  109.3 11.1 %collective-permute-start.8 = (bf16[256,256]{1,0:T(8,128)(2,1)}, bf16[256,256]{1,0:T(8,128)(2,1)}, u32[]{:S(2)}, u32[]{:S(2)}) collective-permute-start(bf16[256,256]{1,0:T(8,128)(2,1)} %get-tuple-element.12), channel_id=1, source_target_pairs={{0,256},{16,272},{32,288},{48,304},{64,320},{80,336},{96,352},{112... | collective-permute-start | bytes 393224 | tf_op jit(solution)/shard_map/ppermute | solution.py:9
  124.8 1.8 %copy-start.3 = (bf16[256,3072]{1,0:T(8,128)(2,1)S(1)}, bf16[256,3072]{1,0:T(8,128)(2,1)}, u32[]{:S(2)}) copy-start(bf16[256,3072]{1,0:T(8,128)(2,1)} %all-gather.2.cloned.1.call-done) | copy-start | bytes 4718596
  124.8 1.8 %copy-start.5 = (bf16[256,256]{1,0:T(8,128)(2,1)S(1)}, bf16[256,256]{1,0:T(8,128)(2,1)}, u32[]{:S(2)}) copy-start(bf16[256,256]{1,0:T(8,128)(2,1)} %convolution_convert_fusion.5) | copy-start | bytes 393220
  126.6 1.0 copy-start.4
  126.6 1.0 copy-start.6
Sparse Core Ops, SparseCore 0:
  24.8 44.6 all-gather.1
